TPU v7x, 128 devices: a whole 4x4x4 slice. The times are simulated.
128 devices in a mesh: tile: 16 (over z, x_hi, core), win: 8 (over y, x_lo).
Axes of the slice: x: 4 (x_hi: 2, x_lo: 2; x = x_hi * 2 + x_lo), y: 4, z: 4, core: 2. Of those that a mesh axis runs over, the one named last changes fastest.
Arguments:
- initial_state: float32 [8, 4, 8, 64, 2048], P('win', None, None, None, 'tile'), may hold values from -6 to 6
- observed: float32 [8, 4, 8, 64, 2048], P('win', None, None, None, 'tile'), may hold values from -6 to 6
- mixing: float32 [8, 64, 2048], P(None, None, 'tile'), may hold values from 0.02 to 0.2
- velocity: float32 [8, 64, 2048], P(None, None, 'tile'), may hold values from 0 to 0.15
- sea_mask: int32 [8, 64, 2048], P(None, None, 'tile'), may hold values 0 or 1
- partner: int32 [2048], P('tile'), may hold values from 0 to 2047, as said below
Outputs:
- state_gradient: float32 [8, 4, 8, 64, 2048], P('win', None, None, None, 'tile')
- mixing_gradient: float32 [8, 64, 2048], P(None, 'win', 'tile')
Inputs may be any that keep to these rules, and one draw needn't show every extreme that they name: partner[i] = (s - i) mod 2048 for one whole number s of each draw, so that partner is its own inverse.
All inputs are finite; a program needn't handle non-finite values. No bound on the sum of `sea_mask` on one device may be relied on, other than what follows from the above.
Results may differ from a plain program's by a relative error of at most 0.00002.
Values sent between devices are 32-bit elements; how exact they have to be, the bound alone decides.
No kernel may reach another device: no remote copies, remote signals or barrier semaphores. Data moves between devices by JAX's collectives and lax.ppermute only.
A program may use at most 128 MiB of HBM per device.

v0:
```python
import jax
import jax.numpy as jnp
from jax import lax
from jax.sharding import PartitionSpec as P

STEPS = 6


def padded_2(cells, sides, width):
    for axis, dim in sides:
        count = lax.axis_size(axis)
        head = lax.slice_in_dim(cells, 0, width, axis=dim)
        tail = lax.slice_in_dim(cells, cells.shape[dim] - width, cells.shape[dim], axis=dim)
        cells = jnp.concatenate(
            [
                lax.ppermute(tail, axis, [(i, (i + 1) % count) for i in range(count)]),
                cells,
                lax.ppermute(head, axis, [((i + 1) % count, i) for i in range(count)]),
            ],
            axis=dim,
        )
    return cells


def passed_along(block, axis, distance):
    devices = range(lax.axis_size(axis))
    route = [(i - distance, i) for i in devices if i - distance in devices]
    return lax.ppermute(block, axis, route)


def passed_along_2(value, axis, steps):
    count = lax.axis_size(axis)
    pairs = [(source, (source + steps) % count) for source in range(count)]
    return lax.ppermute(value, axis, pairs)


def north_south(field, ghost_row):
    north = jnp.concatenate([field[..., 1:, :], ghost_row[..., None, :]], axis=-2)
    south = jnp.concatenate([jnp.zeros_like(field[..., :1, :]), field[..., :-1, :]], axis=-2)
    return (north, south)


def advance(
    centre,
    east,
    west,
    north,
    south,
    mixing,
    velocity,
    wet,
    wet_east,
    wet_west,
    wet_north,
    wet_south,
):
    spread = (
        wet_east * (east - centre)
        + wet_west * (west - centre)
        + wet_north * (north - centre)
        + wet_south * (south - centre)
    )
    return centre + wet * (mixing * spread - velocity * wet_west * (centre - west))


def with_columns(field):
    return padded_2(field, (("tile", 3),), 1)


def fold_ghost(top_rows, partner):
    gathered = lax.all_gather(top_rows, "tile", axis=2, tiled=True)
    return jnp.take(gathered, partner, axis=2)


def body(initial_state, observed, mixing, velocity, sea_mask, partner):
    start = initial_state[0]
    target = observed[0]
    wet = sea_mask.astype(jnp.float32)
    wet_padded = with_columns(wet[None])[0]
    wet_east = wet_padded[..., 2:]
    wet_west = wet_padded[..., :-2]
    wet_fold = fold_ghost(wet[None][:, :, -1, :], partner)[0]
    wet_north, wet_south = north_south(wet, wet_fold)
    window = lax.axis_index("win")

    def local_step(padded, ghost_row, coeff):
        centre = padded[..., 1:-1]
        north, south = north_south(centre, ghost_row)
        return advance(
            centre,
            padded[..., 2:],
            padded[..., :-2],
            north,
            south,
            coeff,
            velocity,
            wet,
            wet_east,
            wet_west,
            wet_north,
            wet_south,
        )

    field = start
    stored = []
    for moment in range(STEPS):
        padded = with_columns(field)
        ghost_row = fold_ghost(field[:, :, -1, :], partner)
        stored.append((padded, ghost_row))
        field = local_step(padded, ghost_row, mixing)
    previous_end = passed_along(field, "win", 1)
    mismatch = jnp.where(window > 0, start - previous_end, jnp.zeros_like(start))
    next_mismatch = passed_along(mismatch, "win", -1)
    adjoint = wet * (field - target) - next_mismatch
    mixing_sum = jnp.zeros_like(mixing)
    for moment in range(STEPS - 1, -1, -1):
        padded, ghost_row = stored[moment]
        _, pullback = jax.vjp(local_step, padded, ghost_row, mixing)
        padded_part, ghost_part, mixing_part = pullback(adjoint)
        mixing_sum = mixing_sum + mixing_part
        from_right = passed_along_2(padded_part[..., 0], "tile", -1)
        from_left = passed_along_2(padded_part[..., -1], "tile", 1)
        adjoint = padded_part[..., 1:-1]
        adjoint = adjoint.at[..., -1].add(from_right)
        adjoint = adjoint.at[..., 0].add(from_left)
        adjoint = adjoint.at[:, :, -1, :].add(fold_ghost(ghost_part, partner))
    state_gradient = adjoint + mismatch
    mixing_gradient = lax.psum_scatter(mixing_sum, "win", scatter_dimension=1, tiled=True)
    return (state_gradient[None], mixing_gradient)


def solution(mesh):
    in_specs = (
        P("win", None, None, None, "tile"),
        P("win", None, None, None, "tile"),
        P(None, None, "tile"),
        P(None, None, "tile"),
        P(None, None, "tile"),
        P("tile"),
    )
    out_specs = (P("win", None, None, None, "tile"), P(None, "win", "tile"))
    return jax.shard_map(body, mesh=mesh, in_specs=in_specs, out_specs=out_specs, check_vma=False)
```

profile of v0, /device:TPU:1, one launch (start us, length us, event | category | flops | bytes accessed | tf_op | source)
XLA Modules:
  0.0 869.9 jit_solution(5114606061097768946)
XLA Ops:
  16.8 5.0 fusion.106
  26.9 26.8 %all-gather.1 = f32[4,8,1,2048]{3,1,2,0:T(8,128)S(1)} all-gather(f32[4,8,1,128]{3,1,2,0:T(8,128)S(1)} %bitcast.138), channel_id=3, replica_groups=mesh['tile'=16,'win'=8] {'tile'}, dimensions={3}, use_global_device_ids=true | all-gather | bytes 278528 | tf_op jit(solution)/shard_map/all_gather | solution.py:71
  56.8 26.0 %all-gather = f32[1,8,1,2048]{1,3,2,0:T(8,128)S(1)} all-gather(f32[1,8,1,128]{1,3,2,0:T(8,128)S(1)} %slice.847), channel_id=2, replica_groups=mesh['tile'=16,'win'=8] {'tile'}, dimensions={3}, use_global_device_ids=true | all-gather | bytes 69632 | tf_op jit(solution)/shard_map/all_gather | solution.py:71
  86.7 6.3 fusion.105
  118.9 21.4 %all-gather.2 = f32[4,8,1,2048]{3,1,2,0:T(8,128)S(1)} all-gather(f32[4,8,1,128]{3,1,2,0:T(8,128)S(1)} %bitcast.139), channel_id=4, replica_groups=mesh['tile'=16,'win'=8] {'tile'}, dimensions={3}, use_global_device_ids=true | all-gather | bytes 278528 | tf_op jit(solution)/shard_map/all_gather | solution.py:71
  154.5 5.2 fusion.53
  163.2 23.8 %all-gather.3 = f32[4,8,1,2048]{3,1,2,0:T(8,128)S(1)} all-gather(f32[4,8,1,128]{3,1,2,0:T(8,128)S(1)} %bitcast.140), channel_id=5, replica_groups=mesh['tile'=16,'win'=8] {'tile'}, dimensions={3}, use_global_device_ids=true | all-gather | bytes 278528 | tf_op jit(solution)/shard_map/all_gather | solution.py:71
  202.3 5.1 fusion.41
  210.9 23.6 %all-gather.4 = f32[4,8,1,2048]{3,1,2,0:T(8,128)S(1)} all-gather(f32[4,8,1,128]{3,1,2,0:T(8,128)S(1)} %bitcast.141), channel_id=6, replica_groups=mesh['tile'=16,'win'=8] {'tile'}, dimensions={3}, use_global_device_ids=true | all-gather | bytes 278528 | tf_op jit(solution)/shard_map/all_gather | solution.py:71
  248.8 5.1 fusion.29
  257.4 23.6 %all-gather.5 = f32[4,8,1,2048]{3,1,2,0:T(8,128)S(1)} all-gather(f32[4,8,1,128]{3,1,2,0:T(8,128)S(1)} %bitcast.142), channel_id=7, replica_groups=mesh['tile'=16,'win'=8] {'tile'}, dimensions={3}, use_global_device_ids=true | all-gather | bytes 278528 | tf_op jit(solution)/shard_map/all_gather | solution.py:71
  296.5 5.1 fusion.17
  305.1 23.6 %all-gather.6 = f32[4,8,1,2048]{3,1,2,0:T(8,128)S(1)} all-gather(f32[4,8,1,128]{3,1,2,0:T(8,128)S(1)} %bitcast.143), channel_id=8, replica_groups=mesh['tile'=16,'win'=8] {'tile'}, dimensions={3}, use_global_device_ids=true | all-gather | bytes 278528 | tf_op jit(solution)/shard_map/all_gather | solution.py:71
  343.0 5.7 fusion.5
  352.0 18.4 %collective-permute-done.14 = f32[4,8,64,128]{3,2,1,0:T(8,128)} collective-permute-done((f32[4,8,64,128]{3,2,1,0:T(8,128)}, f32[4,8,64,128]{3,2,1,0:T(8,128)}, u32[]{:S(2)}, u32[]{:S(2)}) %collective-permute-start.14) | collective-permute-done | bytes 1048608 | tf_op jit(solution)/shard_map/ppermute | solution.py:28
  373.1 22.0 %collective-permute-done.15 = f32[4,8,64,128]{3,2,1,0:T(8,128)S(1)} collective-permute-done((f32[4,8,64,128]{3,2,1,0:T(8,128)S(1)}, f32[4,8,64,128]{3,2,1,0:T(8,128)S(1)}, u32[]{:S(2)}, u32[]{:S(2)}) %collective-permute-start.15) | collective-permute-done | bytes 1048608 | tf_op jit(solution)/shard_map/ppermute | solution.py:28
  397.6 32.6 %all-gather.7 = f32[4,8,1,2048]{3,1,2,0:T(8,128)S(1)} all-gather(f32[4,8,1,128]{3,1,2,0:T(8,128)S(1)} %bitcast.144), channel_id=9, replica_groups=mesh['tile'=16,'win'=8] {'tile'}, dimensions={3}, use_global_device_ids=true | all-gather | bytes 278528 | tf_op jit(solution)/shard_map/all_gather | solution.py:71
  451.7 4.6 scatter-add.60
  465.6 21.0 %all-gather.8 = f32[4,8,1,2048]{3,1,2,0:T(8,128)S(1)} all-gather(f32[4,8,1,128]{3,1,2,0:T(8,128)S(1)} %bitcast.134), channel_id=10, replica_groups=mesh['tile'=16,'win'=8] {'tile'}, dimensions={3}, use_global_device_ids=true | all-gather | bytes 278528 | tf_op jit(solution)/shard_map/all_gather | solution.py:71
  500.2 4.6 scatter-add.65
  515.2 23.7 %all-gather.9 = f32[4,8,1,2048]{3,1,2,0:T(8,128)S(1)} all-gather(f32[4,8,1,128]{3,1,2,0:T(8,128)S(1)} %bitcast.135), channel_id=11, replica_groups=mesh['tile'=16,'win'=8] {'tile'}, dimensions={3}, use_global_device_ids=true | all-gather | bytes 278528 | tf_op jit(solution)/shard_map/all_gather | solution.py:71
  553.7 5.2 scatter-add.70
  574.3 23.6 %all-gather.10 = f32[4,8,1,2048]{3,1,2,0:T(8,128)S(1)} all-gather(f32[4,8,1,128]{3,1,2,0:T(8,128)S(1)} %bitcast.136), channel_id=12, replica_groups=mesh['tile'=16,'win'=8] {'tile'}, dimensions={3}, use_global_device_ids=true | all-gather | bytes 278528 | tf_op jit(solution)/shard_map/all_gather | solution.py:71
  611.9 5.2 scatter-add.75
  632.6 23.6 %all-gather.11 = f32[4,8,1,2048]{3,1,2,0:T(8,128)S(1)} all-gather(f32[4,8,1,128]{3,1,2,0:T(8,128)S(1)} %bitcast.137), channel_id=13, replica_groups=mesh['tile'=16,'win'=8] {'tile'}, dimensions={3}, use_global_device_ids=true | all-gather | bytes 278528 | tf_op jit(solution)/shard_map/all_gather | solution.py:71
  671.4 5.2 scatter-add.80
  685.5 7.2 multiply_reduce_fusion.4
  696.6 23.6 %all-gather.12 = f32[4,8,1,2048]{3,1,2,0:T(8,128)S(1)} all-gather(f32[4,8,1,128]{3,1,2,0:T(8,128)S(1)} %bitcast.133), channel_id=14, replica_groups=mesh['tile'=16,'win'=8] {'tile'}, dimensions={3}, use_global_device_ids=true | all-gather | bytes 278528 | tf_op jit(solution)/shard_map/all_gather | solution.py:71
  732.7 4.5 copy.1467
  750.4 4.5 copy.1472
  754.9 13.9 %add_add_fusion = f32[8,64,128]{0,1,2:T(8,128)} fusion(f32[8,64,128]{0,1,2:T(8,128)} %copy.1472, f32[8,64,128]{0,1,2:T(8,128)} %copy.1471, f32[8,64,128]{0,1,2:T(8,128)} %copy.1470, f32[8,64,128]{0,1,2:T(8,128)} %copy.1469, f32[8,64,128]{0,1,2:T(8,128)} %copy.1467, f32[8,64,128]{0,1,2:T(8,128)} %copy.1468), kind=kLoop, calls=%fused_computation.14 | loop fusion | flops 327680 | bytes 1835008 | tf_op jit(solution)/shard_map/add | solution.py:120
  782.4 78.7 %reduce-scatter.2.cloned.1.call-done = f32[8,8,128]{0,1,2:T(8,128)} async-done(((f32[8,64,128]{0,1,2:T(8,128)}), f32[8,8,128]{0,1,2:T(8,128)}) %reduce-scatter.2.cloned.1.call-update) | async-done | bytes 32784 | tf_op jit(solution)/shard_map/reduce_scatter | solution.py:128
  (311 shorter events, 326.3 us)
Async XLA Ops:
  7.2 853.9 %reduce-scatter.2.cloned.1.call-start = ((), (), s32[]{:S(2)}) async-start(), calls=%async_computation.1 | async-start | bytes 4718592 | tf_op jit(solution)/shard_map/reduce_scatter | solution.py:128
  9.5 100.4 %collective-permute-start.3 = (f32[4,8,64,1]{2,1,3,0:T(8,128)S(1)}, f32[4,8,64,1]{2,1,3,0:T(8,128)S(1)}, u32[]{:S(2)}, u32[]{:S(2)}) collective-permute-start(f32[4,8,64,1]{2,1,3,0:T(8,128)S(1)} %copy.1355), channel_id=1, source_target_pairs={{0,8},{8,16},{16,24},{24,32},{32,40},{40,48},{48,56},{56,64},{64,7... | collective-permute-start | bytes 24584 | tf_op jit(solution)/shard_map/ppermute | solution.py:16
  14.1 94.4 %collective-permute-start.2 = (f32[4,8,64,1]{2,1,3,0:T(8,128)S(1)}, f32[4,8,64,1]{2,1,3,0:T(8,128)S(1)}, u32[]{:S(2)}, u32[]{:S(2)}) collective-permute-start(f32[4,8,64,1]{2,1,3,0:T(8,128)S(1)} %copy.1353), channel_id=1, source_target_pairs={{8,0},{16,8},{24,16},{32,24},{40,32},{48,40},{56,48},{64,56},{72,6... | collective-permute-start | bytes 24584 | tf_op jit(solution)/shard_map/ppermute | solution.py:18
  21.9 85.7 %collective-permute-start = (f32[1,8,64,1]{1,3,2,0:T(1,128)S(1)}, f32[1,8,64,1]{1,3,2,0:T(1,128)S(1)}, u32[]{:S(2)}, u32[]{:S(2)}) collective-permute-start(f32[1,8,64,1]{1,3,2,0:T(1,128)S(1)} %get-tuple-element.279), channel_id=1, source_target_pairs={{0,8},{8,16},{16,24},{24,32},{32,40},{40,48},{48,56},{56,64},{64,7... | collective-permute-start | bytes 6152 | tf_op jit(solution)/shard_map/ppermute | solution.py:16
  25.1 82.0 %collective-permute-start.1 = (f32[1,8,64,1]{1,3,2,0:T(1,128)S(1)}, f32[1,8,64,1]{1,3,2,0:T(1,128)S(1)}, u32[]{:S(2)}, u32[]{:S(2)}) collective-permute-start(f32[1,8,64,1]{1,3,2,0:T(1,128)S(1)} %get-tuple-element.280), channel_id=1, source_target_pairs={{8,0},{16,8},{24,16},{32,24},{40,32},{48,40},{56,48},{64,56},{72,6... | collective-permute-start | bytes 6152 | tf_op jit(solution)/shard_map/ppermute | solution.py:18
  143.4 9.7 %collective-permute-start.5 = (f32[4,8,64,1]{2,1,3,0:T(8,128)S(1)}, f32[4,8,64,1]{2,1,3,0:T(8,128)S(1)}, u32[]{:S(2)}, u32[]{:S(2)}) collective-permute-start(f32[4,8,64,1]{2,1,3,0:T(8,128)S(1)} %copy.1365), channel_id=1, source_target_pairs={{0,8},{8,16},{16,24},{24,32},{32,40},{40,48},{48,56},{56,64},{64,7... | collective-permute-start | bytes 24584 | tf_op jit(solution)/shard_map/ppermute | solution.py:16
  145.2 6.5 collective-permute-start.4
  190.2 10.7 %collective-permute-start.7 = (f32[4,8,64,1]{2,1,3,0:T(8,128)S(1)}, f32[4,8,64,1]{2,1,3,0:T(8,128)S(1)}, u32[]{:S(2)}, u32[]{:S(2)}) collective-permute-start(f32[4,8,64,1]{2,1,3,0:T(8,128)S(1)} %copy.1373), channel_id=1, source_target_pairs={{0,8},{8,16},{16,24},{24,32},{32,40},{40,48},{48,56},{56,64},{64,7... | collective-permute-start | bytes 24584 | tf_op jit(solution)/shard_map/ppermute | solution.py:16
  193.2 6.3 collective-permute-start.6
  237.7 9.7 %collective-permute-start.9 = (f32[4,8,64,1]{2,1,3,0:T(8,128)S(1)}, f32[4,8,64,1]{2,1,3,0:T(8,128)S(1)}, u32[]{:S(2)}, u32[]{:S(2)}) collective-permute-start(f32[4,8,64,1]{2,1,3,0:T(8,128)S(1)} %copy.1381), channel_id=1, source_target_pairs={{0,8},{8,16},{16,24},{24,32},{32,40},{40,48},{48,56},{56,64},{64,7... | collective-permute-start | bytes 24584 | tf_op jit(solution)/shard_map/ppermute | solution.py:16
  239.7 6.3 collective-permute-start.8
  284.2 10.9 %collective-permute-start.11 = (f32[4,8,64,1]{2,1,3,0:T(8,128)S(1)}, f32[4,8,64,1]{2,1,3,0:T(8,128)S(1)}, u32[]{:S(2)}, u32[]{:S(2)}) collective-permute-start(f32[4,8,64,1]{2,1,3,0:T(8,128)S(1)} %copy.1389), channel_id=1, source_target_pairs={{0,8},{8,16},{16,24},{24,32},{32,40},{40,48},{48,56},{56,64},{64,7... | collective-permute-start | bytes 24584 | tf_op jit(solution)/shard_map/ppermute | solution.py:16
  287.1 6.5 collective-permute-start.10
  331.8 9.7 %collective-permute-start.13 = (f32[4,8,64,1]{2,1,3,0:T(8,128)S(1)}, f32[4,8,64,1]{2,1,3,0:T(8,128)S(1)}, u32[]{:S(2)}, u32[]{:S(2)}) collective-permute-start(f32[4,8,64,1]{2,1,3,0:T(8,128)S(1)} %copy.1397), channel_id=1, source_target_pairs={{0,8},{8,16},{16,24},{24,32},{32,40},{40,48},{48,56},{56,64},{64,7... | collective-permute-start | bytes 24584 | tf_op jit(solution)/shard_map/ppermute | solution.py:16
  333.8 6.3 collective-permute-start.12
  348.7 21.7 %collective-permute-start.14 = (f32[4,8,64,128]{3,2,1,0:T(8,128)}, f32[4,8,64,128]{3,2,1,0:T(8,128)}, u32[]{:S(2)}, u32[]{:S(2)}) collective-permute-start(f32[4,8,64,128]{3,2,1,0:T(8,128)} %get-tuple-element.263), channel_id=1, source_target_pairs={{0,1},{1,2},{2,3},{3,4},{4,5},{5,6},{6,7},{8,9},{9,10},{10,11},{11... | collective-permute-start | bytes 3145736 | tf_op jit(solution)/shard_map/ppermute | solution.py:28
  371.8 23.3 %collective-permute-start.15 = (f32[4,8,64,128]{3,2,1,0:T(8,128)S(1)}, f32[4,8,64,128]{3,2,1,0:T(8,128)S(1)}, u32[]{:S(2)}, u32[]{:S(2)}) collective-permute-start(f32[4,8,64,128]{3,2,1,0:T(8,128)S(1)} %subtract_select_fusion), channel_id=1, source_target_pairs={{1,0},{2,1},{3,2},{4,3},{5,4},{6,5},{7,6},{9,8},{10,9},{11,10},{12... | collective-permute-start | bytes 3145736 | tf_op jit(solution)/shard_map/ppermute | solution.py:28
  397.1 33.8 %copy-start.18 = (f32[4,8,64,128]{3,2,1,0:T(8,128)}, f32[4,8,64,128]{3,2,1,0:T(8,128)S(1)}, u32[]{:S(2)}) copy-start(f32[4,8,64,128]{3,2,1,0:T(8,128)S(1)} %get-tuple-element.262) | copy-start | bytes 3145732
  434.4 11.8 %collective-permute-start.16 = (f32[4,8,64]{2,1,0:T(8,128)S(1)}, f32[4,8,64]{2,1,0:T(8,128)S(1)}, u32[]{:S(2)}, u32[]{:S(2)}) collective-permute-start(f32[4,8,64]{2,1,0:T(8,128)S(1)} %get-tuple-element.254), channel_id=1, source_target_pairs={{0,120},{8,0},{16,8},{24,16},{32,24},{40,32},{48,40},{56,48},{64,5... | collective-permute-start | bytes 24584 | tf_op jit(solution)/shard_map/ppermute | solution.py:34
  442.7 7.6 collective-permute-start.17
  486.6 12.2 %collective-permute-start.19 = (f32[4,8,64]{2,1,0:T(8,128)S(1)}, f32[4,8,64]{2,1,0:T(8,128)S(1)}, u32[]{:S(2)}, u32[]{:S(2)}) collective-permute-start(f32[4,8,64]{2,1,0:T(8,128)S(1)} %get-tuple-element.251), channel_id=1, source_target_pairs={{0,8},{8,16},{16,24},{24,32},{32,40},{40,48},{48,56},{56,64},{64,7... | collective-permute-start | bytes 24584 | tf_op jit(solution)/shard_map/ppermute | solution.py:34
  488.3 6.3 collective-permute-start.18
  538.9 13.4 %collective-permute-start.21 = (f32[4,8,64]{2,1,0:T(8,128)S(1)}, f32[4,8,64]{2,1,0:T(8,128)S(1)}, u32[]{:S(2)}, u32[]{:S(2)}) collective-permute-start(f32[4,8,64]{2,1,0:T(8,128)S(1)} %get-tuple-element.249), channel_id=1, source_target_pairs={{0,8},{8,16},{16,24},{24,32},{32,40},{40,48},{48,56},{56,64},{64,7... | collective-permute-start | bytes 24584 | tf_op jit(solution)/shard_map/ppermute | solution.py:34
  541.8 6.3 collective-permute-start.20
  597.9 12.6 %collective-permute-start.23 = (f32[4,8,64]{2,1,0:T(8,128)S(1)}, f32[4,8,64]{2,1,0:T(8,128)S(1)}, u32[]{:S(2)}, u32[]{:S(2)}) collective-permute-start(f32[4,8,64]{2,1,0:T(8,128)S(1)} %get-tuple-element.247), channel_id=1, source_target_pairs={{0,8},{8,16},{16,24},{24,32},{32,40},{40,48},{48,56},{56,64},{64,7... | collective-permute-start | bytes 24584 | tf_op jit(solution)/shard_map/ppermute | solution.py:34
  599.8 6.5 collective-permute-start.22
  656.2 13.8 %collective-permute-start.25 = (f32[4,8,64]{2,1,0:T(8,128)S(1)}, f32[4,8,64]{2,1,0:T(8,128)S(1)}, u32[]{:S(2)}, u32[]{:S(2)}) collective-permute-start(f32[4,8,64]{2,1,0:T(8,128)S(1)} %get-tuple-element.245), channel_id=1, source_target_pairs={{0,8},{8,16},{16,24},{24,32},{32,40},{40,48},{48,56},{56,64},{64,7... | collective-permute-start | bytes 24584 | tf_op jit(solution)/shard_map/ppermute | solution.py:34
  659.1 6.7 collective-permute-start.24
  694.9 33.4 %copy-start.23 = (f32[8,64,128]{2,1,0:T(8,128)S(1)}, f32[8,64,128]{2,1,0:T(8,128)}, u32[]{:S(2)}) copy-start(f32[8,64,128]{2,1,0:T(8,128)} %get-tuple-element.255) | copy-start | bytes 786436
  720.2 52.0 %collective-permute-start.27 = (f32[4,8,64]{2,1,0:T(8,128)S(1)}, f32[4,8,64]{2,1,0:T(8,128)S(1)}, u32[]{:S(2)}, u32[]{:S(2)}) collective-permute-start(f32[4,8,64]{2,1,0:T(8,128)S(1)} %get-tuple-element.243), channel_id=1, source_target_pairs={{0,8},{8,16},{16,24},{24,32},{32,40},{40,48},{48,56},{56,64},{64,7... | collective-permute-start | bytes 24584 | tf_op jit(solution)/shard_map/ppermute | solution.py:34
  722.1 47.0 %collective-permute-start.26 = (f32[4,8,64]{2,1,0:T(8,128)S(1)}, f32[4,8,64]{2,1,0:T(8,128)S(1)}, u32[]{:S(2)}, u32[]{:S(2)}) collective-permute-start(f32[4,8,64]{2,1,0:T(8,128)S(1)} %get-tuple-element.244), channel_id=1, source_target_pairs={{0,120},{8,0},{16,8},{24,16},{32,24},{40,32},{48,40},{56,48},{64,5... | collective-permute-start | bytes 24584 | tf_op jit(solution)/shard_map/ppermute | solution.py:34
  722.3 10.5 %copy-start.22 = (f32[8,64,128]{2,1,0:T(8,128)S(1)}, f32[8,64,128]{2,1,0:T(8,128)}, u32[]{:S(2)}) copy-start(f32[8,64,128]{2,1,0:T(8,128)} %get-tuple-element.256) | copy-start | bytes 786436
  (24 other events, 96.8 us)
Sparse Core Ops, SparseCore 0:
  769.2 91.7 reduce-scatter.1
where the time goes:
time: 880 us; the launch traced here: 870 us
  blocking collectives  317 us (36%)
  local copies, waits for them, and re-layouts  262 us (30%)
  waiting for transfers between devices  119 us (14%)
  other arithmetic  116 us (13%)
  starting transfers between devices  40.3 us (5%)
  between operations  15.2 us (2%)
    all_gather x13, blocking collectives, fold_ghost(): gathered = lax.all_gather(top_rows, 'tile', axis=2, tiled=True)  317 us
    reduce_scatter x1, waiting for transfers between devices, body(): lax.psum_scatter(mixing_sum, 'win', scatter_dimension=1, tiled=True)  78.7 us
    ppermute x2, waiting for transfers between devices, passed_along(): return lax.ppermute(block, axis, route)  40.4 us
    unnamed x63, local copies, waits for them, and re-layouts  37.6 us
    all_gather x12, local copies, waits for them, and re-layouts, fold_ghost(): gathered = lax.all_gather(top_rows, 'tile', axis=2, tiled=True)  36.9 us
    gather x14, local copies, waits for them, and re-layouts, fold_ghost(): return jnp.take(gathered, partner, axis=2)  36.1 us
    add x6, other arithmetic, advance(): centre + wet * (mixing * spread - velocity * wet_west * (centre - west))  30.6 us
    scatter-add x6, local copies, waits for them, and re-layouts, body(): adjoint = adjoint.at[..., -1].add(from_right)  28.5 us
  transfers between devices with their start and end apart: 29, of which 3 were waited for; matrix products, arithmetic and copies ran while one was open for 22% of the time, Pallas kernels for 0%

commit v1 on v0

--- a/solution.py
+++ b/solution.py
@@ -68,7 +68,10 @@
 
 
 def fold_ghost(top_rows, partner):
-    gathered = lax.all_gather(top_rows, "tile", axis=2, tiled=True)
+    devices_2 = lax.axis_size("tile")
+    tiles = jnp.stack([top_rows for _ in range(devices_2)])
+    tiles = lax.all_to_all(tiles, "tile", split_axis=0, concat_axis=0)
+    gathered = jnp.concatenate(tiles, axis=2)
     return jnp.take(gathered, partner, axis=2)
 
 

time: 880 us -> 733 us (0.83)
  blocking collectives: 317 us -> 0 us
  local copies, waits for them, and re-layouts: 262 us -> 392 us
  starting transfers between devices: 40.3 us -> 144 us
  waiting for transfers between devices: 119 us -> 71 us
  other arithmetic: 116 us -> 95.2 us
    all_gather x13 -> x0, blocking collectives: 317 us -> none  [fold_ghost(): gathered = lax.all_gather(top_rows, 'tile', axis=2, tiled=True)]
    scatter-add x6, local copies, waits for them, and re-layouts: 28.5 us -> 130 us  [body(): adjoint = adjoint.at[..., -1].add(from_right)]
    all_to_all x0 -> x13, starting transfers between devices: none -> 98 us  [fold_ghost(): tiles = lax.all_to_all(tiles, 'tile', split_axis=0, concat_axis=0)]
    reduce_scatter x1, waiting for transfers between devices: 78.7 us -> 0.01 us  [body(): lax.psum_scatter(mixing_sum, 'win', scatter_dimension=1, tiled=True)]
    reshape x0 -> x13, local copies, waits for them, and re-layouts: none -> 38 us  [fold_ghost(): gathered = jnp.concatenate(tiles, axis=2)]
    all_gather x12 -> x0, local copies, waits for them, and re-layouts: 36.9 us -> none  [fold_ghost(): gathered = lax.all_gather(top_rows, 'tile', axis=2, tiled=True)]
    unnamed x63 -> x75, local copies, waits for them, and re-layouts: 37.6 us -> 13.4 us
    another operation x17 -> x37, local copies, waits for them, and re-layouts: 17.3 us -> 35 us
  transfers between devices with their start and end apart: 29 -> 42, of which waited for: 3 -> 9; matrix products, arithmetic and copies ran while one was open for 22% -> 42% of each run, Pallas kernels for 0% -> 0%
where the time goes in v1:
time: 733 us; the launch traced here: 718 us
  local copies, waits for them, and re-layouts  392 us (53%)
  starting transfers between devices  144 us (20%)
  other arithmetic  95.2 us (13%)
  waiting for transfers between devices  71 us (10%)
  between operations  15.6 us (2%)
    scatter-add x6, local copies, waits for them, and re-layouts, body(): adjoint = adjoint.at[..., -1].add(from_right)  130 us
    all_to_all x13, starting transfers between devices, fold_ghost(): tiles = lax.all_to_all(tiles, 'tile', split_axis=0, concat_axis=0)  98 us
    ppermute x2, waiting for transfers between devices, passed_along(): return lax.ppermute(block, axis, route)  49.1 us
    reshape x13, local copies, waits for them, and re-layouts, fold_ghost(): gathered = jnp.concatenate(tiles, axis=2)  38 us
    gather x13, local copies, waits for them, and re-layouts, fold_ghost(): return jnp.take(gathered, partner, axis=2)  37.3 us
    scatter-add x6, local copies, waits for them, and re-layouts, body(): adjoint = adjoint.at[..., 0].add(from_left)  26.4 us
    add x6, other arithmetic, advance(): centre + wet * (mixing * spread - velocity * wet_west * (centre - west))  25.7 us
    ppermute x7, starting transfers between devices, padded_2(): lax.ppermute(tail, axis, [(i, (i + 1) % count) for i in range(count)])  22.2 us
  transfers between devices with their start and end apart: 42, of which 9 were waited for; matrix products, arithmetic and copies ran while one was open for 42% of the time, Pallas kernels for 0%

profile of v1, /device:TPU:1, one launch (start us, length us, event | category | flops | bytes accessed | tf_op | source)
XLA Modules:
  0.0 718.5 jit_solution(13161174651971371311)
XLA Ops:
  8.8 9.3 %all-to-all-start = ((f32[16,1,8,128]{3,2,1,0:T(8,128)}), f32[16,1,8,128]{3,2,1,0:T(8,128)S(1)}, u32[]{:S(2)}, u32[]{:S(2)}) async-start(f32[16,1,8,128]{3,2,1,0:T(8,128)} %stack.38), calls=%async_computation | async-start | bytes 131072 | tf_op jit(solution)/shard_map/all_to_all | solution.py:73
  42.4 7.8 %all-to-all-start.1 = ((f32[16,4,8,128]{3,2,1,0:T(8,128)}), f32[16,4,8,128]{3,2,1,0:T(8,128)S(1)}, u32[]{:S(2)}, u32[]{:S(2)}) async-start(f32[16,4,8,128]{3,2,1,0:T(8,128)} %stack.39), calls=%async_computation.1 | async-start | bytes 524288 | tf_op jit(solution)/shard_map/all_to_all | solution.py:73
  53.8 5.1 all-to-all-done.1
  71.8 4.4 all-to-all-start.2
  97.8 4.2 fusion.53
  104.4 6.1 all-to-all-start.3
  131.8 4.3 fusion.41
  138.5 6.0 all-to-all-start.4
  166.2 4.2 fusion.29
  172.8 6.0 all-to-all-start.5
  200.2 4.2 fusion.17
  206.8 6.0 all-to-all-start.6
  234.2 4.6 fusion.5
  241.1 22.9 %collective-permute-done.14 = f32[4,8,64,128]{3,1,0,2:T(8,128)S(1)} collective-permute-done((f32[4,8,64,128]{3,1,0,2:T(8,128)}, f32[4,8,64,128]{3,1,0,2:T(8,128)S(1)}, u32[]{:S(2)}, u32[]{:S(2)}) %collective-permute-start.14) | collective-permute-done | bytes 1048608 | tf_op jit(solution)/shard_map/ppermute | solution.py:28
  267.3 26.2 %collective-permute-done.15 = f32[4,8,64,128]{3,1,0,2:T(8,128)S(1)} collective-permute-done((f32[4,8,64,128]{3,1,0,2:T(8,128)S(1)}, f32[4,8,64,128]{3,1,0,2:T(8,128)S(1)}, u32[]{:S(2)}, u32[]{:S(2)}) %collective-permute-start.15) | collective-permute-done | bytes 1048608 | tf_op jit(solution)/shard_map/ppermute | solution.py:28
  309.8 7.1 all-to-all-start.7
  323.3 21.5 %scatter-add.60 = f32[4,8,64,128]{3,1,0,2:T(8,128)S(1)} dynamic-update-slice(f32[4,8,64,128]{3,1,0,2:T(8,128)S(1)} %slice.877, f32[4,8,64,1]{3,1,0,2:T(8,128)} %slice_add_fusion.11, s32[]{:T(128)} %constant.410.clone.1, s32[]{:T(128)} %constant.410.clone.1, s32[]{:T(128)} %constant.410.clone.1, s32[]{:T(128)} %constant.416.clone.1) | dynamic-update-slice | bytes 16388 | tf_op jit(solution)/shard_map/scatter-add | solution.py:127
  374.1 9.3 %all-to-all-start.8 = ((f32[16,4,8,128]{3,2,1,0:T(8,128)}), f32[16,4,8,128]{3,2,1,0:T(8,128)S(1)}, u32[]{:S(2)}, u32[]{:S(2)}) async-start(f32[16,4,8,128]{3,2,1,0:T(8,128)} %stack.48), calls=%async_computation.8 | async-start | bytes 524288 | tf_op jit(solution)/shard_map/all_to_all | solution.py:73
  389.8 22.0 %scatter-add.65 = f32[4,8,64,128]{3,1,0,2:T(8,128)} dynamic-update-slice(f32[4,8,64,128]{3,1,0,2:T(8,128)} %slice.883, f32[4,8,64,1]{3,1,0,2:T(8,128)} %slice_add_fusion.9, s32[]{:T(128)} %constant.410.clone.1, s32[]{:T(128)} %constant.410.clone.1, s32[]{:T(128)} %constant.410.clone.1, s32[]{:T(128)} %constant.416.clone.1) | dynamic-update-slice | bytes 16388 | tf_op jit(solution)/shard_map/scatter-add | solution.py:127
  414.5 4.7 scatter-add.66
  445.1 9.0 %all-to-all-start.9 = ((f32[16,4,8,128]{3,2,1,0:T(8,128)}), f32[16,4,8,128]{3,2,1,0:T(8,128)S(1)}, u32[]{:S(2)}, u32[]{:S(2)}) async-start(f32[16,4,8,128]{3,2,1,0:T(8,128)} %stack.50), calls=%async_computation.9 | async-start | bytes 524288 | tf_op jit(solution)/shard_map/all_to_all | solution.py:73
  460.6 22.0 %scatter-add.70 = f32[4,8,64,128]{3,1,0,2:T(8,128)} dynamic-update-slice(f32[4,8,64,128]{3,1,0,2:T(8,128)} %slice.889, f32[4,8,64,1]{3,1,0,2:T(8,128)} %slice_add_fusion.7, s32[]{:T(128)} %constant.410.clone.1, s32[]{:T(128)} %constant.410.clone.1, s32[]{:T(128)} %constant.410.clone.1, s32[]{:T(128)} %constant.416.clone.1) | dynamic-update-slice | bytes 16388 | tf_op jit(solution)/shard_map/scatter-add | solution.py:127
  485.3 4.7 scatter-add.71
  516.1 9.1 %all-to-all-start.10 = ((f32[16,4,8,128]{3,2,1,0:T(8,128)}), f32[16,4,8,128]{3,2,1,0:T(8,128)S(1)}, u32[]{:S(2)}, u32[]{:S(2)}) async-start(f32[16,4,8,128]{3,2,1,0:T(8,128)} %stack.52), calls=%async_computation.10 | async-start | bytes 524288 | tf_op jit(solution)/shard_map/all_to_all | solution.py:73
  531.5 22.0 %scatter-add.75 = f32[4,8,64,128]{3,1,0,2:T(8,128)} dynamic-update-slice(f32[4,8,64,128]{3,1,0,2:T(8,128)} %slice.895, f32[4,8,64,1]{3,1,0,2:T(8,128)} %slice_add_fusion.5, s32[]{:T(128)} %constant.410.clone.1, s32[]{:T(128)} %constant.410.clone.1, s32[]{:T(128)} %constant.410.clone.1, s32[]{:T(128)} %constant.416.clone.1) | dynamic-update-slice | bytes 16388 | tf_op jit(solution)/shard_map/scatter-add | solution.py:127
  556.3 4.7 scatter-add.76
  586.9 8.8 %all-to-all-start.11 = ((f32[16,4,8,128]{3,2,1,0:T(8,128)}), f32[16,4,8,128]{3,2,1,0:T(8,128)S(1)}, u32[]{:S(2)}, u32[]{:S(2)}) async-start(f32[16,4,8,128]{3,2,1,0:T(8,128)} %stack.54), calls=%async_computation.11 | async-start | bytes 524288 | tf_op jit(solution)/shard_map/all_to_all | solution.py:73
  602.4 22.0 %scatter-add.80 = f32[4,8,64,128]{3,1,0,2:T(8,128)} dynamic-update-slice(f32[4,8,64,128]{3,1,0,2:T(8,128)} %slice.901, f32[4,8,64,1]{3,1,0,2:T(8,128)} %slice_add_fusion.3, s32[]{:T(128)} %constant.410.clone.1, s32[]{:T(128)} %constant.410.clone.1, s32[]{:T(128)} %constant.410.clone.1, s32[]{:T(128)} %constant.416.clone.1) | dynamic-update-slice | bytes 16388 | tf_op jit(solution)/shard_map/scatter-add | solution.py:127
  627.1 4.7 scatter-add.81
  639.5 7.4 %multiply_reduce_fusion.4 = (f32[8,64,128]{2,0,1:T(8,128)S(1)}, f32[8,64,128]{2,0,1:T(8,128)S(1)}, f32[8,64,128]{2,0,1:T(8,128)}, f32[8,64,128]{2,0,1:T(8,128)},...) fusion(f32[4,8,64,128]{3,1,0,2:T(8,128)} %get-tuple-element.250, ...), kind=kLoop, calls=%fused_computation.135 | loop fusion | flops 5111808 | bytes 17301504 | tf_op jit(solution)/shard_map/transpose(jvp())/reduce_sum | solution.py:63
  661.4 9.1 %all-to-all-start.12 = ((f32[16,4,8,128]{3,2,1,0:T(8,128)}), f32[16,4,8,128]{3,2,1,0:T(8,128)S(1)}, u32[]{:S(2)}, u32[]{:S(2)}) async-start(f32[16,4,8,128]{3,2,1,0:T(8,128)} %stack.56), calls=%async_computation.12 | async-start | bytes 524288 | tf_op jit(solution)/shard_map/all_to_all | solution.py:73
  676.0 20.7 %scatter-add.85 = f32[4,8,64,128]{3,1,0,2:T(8,128)S(1)} dynamic-update-slice(f32[4,8,64,128]{3,1,0,2:T(8,128)S(1)} %slice.907, f32[4,8,64,1]{3,1,0,2:T(8,128)S(1)} %slice_add_fusion.1, s32[]{:T(128)} %constant.410.clone.1, s32[]{:T(128)} %constant.410.clone.1, s32[]{:T(128)} %constant.410.clone.1, s32[]{:T(128)} %constant.416.clone.1) | dynamic-update-slice | bytes 16388 | tf_op jit(solution)/shard_map/scatter-add | solution.py:127
  (363 shorter events, 372.7 us)
Async XLA Ops:
  8.8 32.8 %all-to-all-start = ((f32[16,1,8,128]{3,2,1,0:T(8,128)}), f32[16,1,8,128]{3,2,1,0:T(8,128)S(1)}, u32[]{:S(2)}, u32[]{:S(2)}) async-start(f32[16,1,8,128]{3,2,1,0:T(8,128)} %stack.38), calls=%async_computation | async-start | bytes 131072 | tf_op jit(solution)/shard_map/all_to_all | solution.py:73
  19.0 15.9 %collective-permute-start = (f32[1,8,64,1]{3,2,1,0:T(8,128)}, f32[1,8,64,1]{3,2,1,0:T(8,128)S(1)}, u32[]{:S(2)}, u32[]{:S(2)}) collective-permute-start(f32[1,8,64,1]{3,2,1,0:T(8,128)} %get-tuple-element.333), channel_id=1, source_target_pairs={{0,8},{8,16},{16,24},{24,32},{32,40},{40,48},{48,56},{56,64},{64,7... | collective-permute-start | bytes 6152 | tf_op jit(solution)/shard_map/ppermute | solution.py:16
  22.1 12.8 %collective-permute-start.1 = (f32[1,8,64,1]{3,2,1,0:T(8,128)S(1)}, f32[1,8,64,1]{3,2,1,0:T(8,128)S(1)}, u32[]{:S(2)}, u32[]{:S(2)}) collective-permute-start(f32[1,8,64,1]{3,2,1,0:T(8,128)S(1)} %get-tuple-element.334), channel_id=1, source_target_pairs={{8,0},{16,8},{24,16},{32,24},{40,32},{48,40},{56,48},{64,56},{72,6... | collective-permute-start | bytes 6152 | tf_op jit(solution)/shard_map/ppermute | solution.py:18
  27.4 12.4 %collective-permute-start.3 = (f32[4,8,64,1]{2,1,3,0:T(8,128)S(1)}, f32[4,8,64,1]{2,1,3,0:T(8,128)S(1)}, u32[]{:S(2)}, u32[]{:S(2)}) collective-permute-start(f32[4,8,64,1]{2,1,3,0:T(8,128)S(1)} %copy.1084), channel_id=1, source_target_pairs={{0,8},{8,16},{16,24},{24,32},{32,40},{40,48},{48,56},{56,64},{64,7... | collective-permute-start | bytes 24584 | tf_op jit(solution)/shard_map/ppermute | solution.py:16
  42.4 16.5 %all-to-all-start.1 = ((f32[16,4,8,128]{3,2,1,0:T(8,128)}), f32[16,4,8,128]{3,2,1,0:T(8,128)S(1)}, u32[]{:S(2)}, u32[]{:S(2)}) async-start(f32[16,4,8,128]{3,2,1,0:T(8,128)} %stack.39), calls=%async_computation.1 | async-start | bytes 524288 | tf_op jit(solution)/shard_map/all_to_all | solution.py:73
  71.8 19.7 %all-to-all-start.2 = ((f32[16,4,8,128]{3,2,1,0:T(8,128)}), f32[16,4,8,128]{3,2,1,0:T(8,128)S(1)}, u32[]{:S(2)}, u32[]{:S(2)}) async-start(f32[16,4,8,128]{3,2,1,0:T(8,128)} %stack.40), calls=%async_computation.2 | async-start | bytes 524288 | tf_op jit(solution)/shard_map/all_to_all | solution.py:73
  104.4 21.1 %all-to-all-start.3 = ((f32[16,4,8,128]{3,2,1,0:T(8,128)}), f32[16,4,8,128]{3,2,1,0:T(8,128)S(1)}, u32[]{:S(2)}, u32[]{:S(2)}) async-start(f32[16,4,8,128]{3,2,1,0:T(8,128)} %stack.41), calls=%async_computation.3 | async-start | bytes 524288 | tf_op jit(solution)/shard_map/all_to_all | solution.py:73
  138.5 21.4 %all-to-all-start.4 = ((f32[16,4,8,128]{3,2,1,0:T(8,128)}), f32[16,4,8,128]{3,2,1,0:T(8,128)S(1)}, u32[]{:S(2)}, u32[]{:S(2)}) async-start(f32[16,4,8,128]{3,2,1,0:T(8,128)} %stack.42), calls=%async_computation.4 | async-start | bytes 524288 | tf_op jit(solution)/shard_map/all_to_all | solution.py:73
  148.1 10.0 %collective-permute-start.9 = (f32[4,8,64,1]{2,1,3,0:T(8,128)S(1)}, f32[4,8,64,1]{2,1,3,0:T(8,128)S(1)}, u32[]{:S(2)}, u32[]{:S(2)}) collective-permute-start(f32[4,8,64,1]{2,1,3,0:T(8,128)S(1)} %copy.1109), channel_id=1, source_target_pairs={{0,8},{8,16},{16,24},{24,32},{32,40},{40,48},{48,56},{56,64},{64,7... | collective-permute-start | bytes 24584 | tf_op jit(solution)/shard_map/ppermute | solution.py:16
  172.8 21.0 %all-to-all-start.5 = ((f32[16,4,8,128]{3,2,1,0:T(8,128)}), f32[16,4,8,128]{3,2,1,0:T(8,128)S(1)}, u32[]{:S(2)}, u32[]{:S(2)}) async-start(f32[16,4,8,128]{3,2,1,0:T(8,128)} %stack.43), calls=%async_computation.5 | async-start | bytes 524288 | tf_op jit(solution)/shard_map/all_to_all | solution.py:73
  206.8 21.2 %all-to-all-start.6 = ((f32[16,4,8,128]{3,2,1,0:T(8,128)}), f32[16,4,8,128]{3,2,1,0:T(8,128)S(1)}, u32[]{:S(2)}, u32[]{:S(2)}) async-start(f32[16,4,8,128]{3,2,1,0:T(8,128)} %stack.44), calls=%async_computation.6 | async-start | bytes 524288 | tf_op jit(solution)/shard_map/all_to_all | solution.py:73
  238.9 25.2 %collective-permute-start.14 = (f32[4,8,64,128]{3,1,0,2:T(8,128)}, f32[4,8,64,128]{3,1,0,2:T(8,128)S(1)}, u32[]{:S(2)}, u32[]{:S(2)}) collective-permute-start(f32[4,8,64,128]{3,1,0,2:T(8,128)} %get-tuple-element.247), channel_id=1, source_target_pairs={{0,1},{1,2},{2,3},{3,4},{4,5},{5,6},{6,7},{8,9},{9,10},{10,11},{11... | collective-permute-start | bytes 3145736 | tf_op jit(solution)/shard_map/ppermute | solution.py:28
  266.0 27.5 %collective-permute-start.15 = (f32[4,8,64,128]{3,1,0,2:T(8,128)S(1)}, f32[4,8,64,128]{3,1,0,2:T(8,128)S(1)}, u32[]{:S(2)}, u32[]{:S(2)}) collective-permute-start(f32[4,8,64,128]{3,1,0,2:T(8,128)S(1)} %subtract_select_fusion), channel_id=1, source_target_pairs={{1,0},{2,1},{3,2},{4,3},{5,4},{6,5},{7,6},{9,8},{10,9},{11,10},{12... | collective-permute-start | bytes 3145736 | tf_op jit(solution)/shard_map/ppermute | solution.py:28
  303.9 14.9 %collective-permute-start.16 = (f32[4,8,64]{2,1,0:T(8,128)S(1)}, f32[4,8,64]{2,1,0:T(8,128)S(1)}, u32[]{:S(2)}, u32[]{:S(2)}) collective-permute-start(f32[4,8,64]{2,1,0:T(8,128)S(1)} %bitcast.181), channel_id=1, source_target_pairs={{0,120},{8,0},{16,8},{24,16},{32,24},{40,32},{48,40},{56,48},{64,5... | collective-permute-start | bytes 24584 | tf_op jit(solution)/shard_map/ppermute | solution.py:34
  304.6 12.4 %collective-permute-start.17 = (f32[4,8,64]{2,1,0:T(8,128)S(1)}, f32[4,8,64]{2,1,0:T(8,128)S(1)}, u32[]{:S(2)}, u32[]{:S(2)}) collective-permute-start(f32[4,8,64]{2,1,0:T(8,128)S(1)} %bitcast.190), channel_id=1, source_target_pairs={{0,8},{8,16},{16,24},{24,32},{32,40},{40,48},{48,56},{56,64},{64,7... | collective-permute-start | bytes 24584 | tf_op jit(solution)/shard_map/ppermute | solution.py:34
  309.8 41.4 %all-to-all-start.7 = ((f32[16,4,8,128]{3,2,1,0:T(8,128)}), f32[16,4,8,128]{3,2,1,0:T(8,128)S(1)}, u32[]{:S(2)}, u32[]{:S(2)}) async-start(f32[16,4,8,128]{3,2,1,0:T(8,128)} %stack.46), calls=%async_computation.7 | async-start | bytes 524288 | tf_op jit(solution)/shard_map/all_to_all | solution.py:73
  366.5 18.7 %collective-permute-start.18 = (f32[4,8,64]{2,1,0:T(8,128)S(1)}, f32[4,8,64]{2,1,0:T(8,128)S(1)}, u32[]{:S(2)}, u32[]{:S(2)}) collective-permute-start(f32[4,8,64]{2,1,0:T(8,128)S(1)} %bitcast.183), channel_id=1, source_target_pairs={{0,120},{8,0},{16,8},{24,16},{32,24},{40,32},{48,40},{56,48},{64,5... | collective-permute-start | bytes 24584 | tf_op jit(solution)/shard_map/ppermute | solution.py:34
  366.5 16.9 %collective-permute-start.19 = (f32[4,8,64]{2,1,0:T(8,128)S(1)}, f32[4,8,64]{2,1,0:T(8,128)S(1)}, u32[]{:S(2)}, u32[]{:S(2)}) collective-permute-start(f32[4,8,64]{2,1,0:T(8,128)S(1)} %bitcast.191), channel_id=1, source_target_pairs={{0,8},{8,16},{16,24},{24,32},{32,40},{40,48},{48,56},{56,64},{64,7... | collective-permute-start | bytes 24584 | tf_op jit(solution)/shard_map/ppermute | solution.py:34
  374.1 45.1 %all-to-all-start.8 = ((f32[16,4,8,128]{3,2,1,0:T(8,128)}), f32[16,4,8,128]{3,2,1,0:T(8,128)S(1)}, u32[]{:S(2)}, u32[]{:S(2)}) async-start(f32[16,4,8,128]{3,2,1,0:T(8,128)} %stack.48), calls=%async_computation.8 | async-start | bytes 524288 | tf_op jit(solution)/shard_map/all_to_all | solution.py:73
  437.5 18.5 %collective-permute-start.20 = (f32[4,8,64]{2,1,0:T(8,128)S(1)}, f32[4,8,64]{2,1,0:T(8,128)S(1)}, u32[]{:S(2)}, u32[]{:S(2)}) collective-permute-start(f32[4,8,64]{2,1,0:T(8,128)S(1)} %bitcast.185), channel_id=1, source_target_pairs={{0,120},{8,0},{16,8},{24,16},{32,24},{40,32},{48,40},{56,48},{64,5... | collective-permute-start | bytes 24584 | tf_op jit(solution)/shard_map/ppermute | solution.py:34
  437.5 16.6 %collective-permute-start.21 = (f32[4,8,64]{2,1,0:T(8,128)S(1)}, f32[4,8,64]{2,1,0:T(8,128)S(1)}, u32[]{:S(2)}, u32[]{:S(2)}) collective-permute-start(f32[4,8,64]{2,1,0:T(8,128)S(1)} %bitcast.192), channel_id=1, source_target_pairs={{0,8},{8,16},{16,24},{24,32},{32,40},{40,48},{48,56},{56,64},{64,7... | collective-permute-start | bytes 24584 | tf_op jit(solution)/shard_map/ppermute | solution.py:34
  445.1 44.9 %all-to-all-start.9 = ((f32[16,4,8,128]{3,2,1,0:T(8,128)}), f32[16,4,8,128]{3,2,1,0:T(8,128)S(1)}, u32[]{:S(2)}, u32[]{:S(2)}) async-start(f32[16,4,8,128]{3,2,1,0:T(8,128)} %stack.50), calls=%async_computation.9 | async-start | bytes 524288 | tf_op jit(solution)/shard_map/all_to_all | solution.py:73
  508.4 18.6 %collective-permute-start.22 = (f32[4,8,64]{2,1,0:T(8,128)S(1)}, f32[4,8,64]{2,1,0:T(8,128)S(1)}, u32[]{:S(2)}, u32[]{:S(2)}) collective-permute-start(f32[4,8,64]{2,1,0:T(8,128)S(1)} %bitcast.187), channel_id=1, source_target_pairs={{0,120},{8,0},{16,8},{24,16},{32,24},{40,32},{48,40},{56,48},{64,5... | collective-permute-start | bytes 24584 | tf_op jit(solution)/shard_map/ppermute | solution.py:34
  508.4 16.7 %collective-permute-start.23 = (f32[4,8,64]{2,1,0:T(8,128)S(1)}, f32[4,8,64]{2,1,0:T(8,128)S(1)}, u32[]{:S(2)}, u32[]{:S(2)}) collective-permute-start(f32[4,8,64]{2,1,0:T(8,128)S(1)} %bitcast.193), channel_id=1, source_target_pairs={{0,8},{8,16},{16,24},{24,32},{32,40},{40,48},{48,56},{56,64},{64,7... | collective-permute-start | bytes 24584 | tf_op jit(solution)/shard_map/ppermute | solution.py:34
  516.1 44.9 %all-to-all-start.10 = ((f32[16,4,8,128]{3,2,1,0:T(8,128)}), f32[16,4,8,128]{3,2,1,0:T(8,128)S(1)}, u32[]{:S(2)}, u32[]{:S(2)}) async-start(f32[16,4,8,128]{3,2,1,0:T(8,128)} %stack.52), calls=%async_computation.10 | async-start | bytes 524288 | tf_op jit(solution)/shard_map/all_to_all | solution.py:73
  579.3 18.5 %collective-permute-start.24 = (f32[4,8,64]{2,1,0:T(8,128)S(1)}, f32[4,8,64]{2,1,0:T(8,128)S(1)}, u32[]{:S(2)}, u32[]{:S(2)}) collective-permute-start(f32[4,8,64]{2,1,0:T(8,128)S(1)} %bitcast.179), channel_id=1, source_target_pairs={{0,120},{8,0},{16,8},{24,16},{32,24},{40,32},{48,40},{56,48},{64,5... | collective-permute-start | bytes 24584 | tf_op jit(solution)/shard_map/ppermute | solution.py:34
  579.3 16.7 %collective-permute-start.25 = (f32[4,8,64]{2,1,0:T(8,128)S(1)}, f32[4,8,64]{2,1,0:T(8,128)S(1)}, u32[]{:S(2)}, u32[]{:S(2)}) collective-permute-start(f32[4,8,64]{2,1,0:T(8,128)S(1)} %bitcast.189), channel_id=1, source_target_pairs={{0,8},{8,16},{16,24},{24,32},{32,40},{40,48},{48,56},{56,64},{64,7... | collective-permute-start | bytes 24584 | tf_op jit(solution)/shard_map/ppermute | solution.py:34
  586.9 44.9 %all-to-all-start.11 = ((f32[16,4,8,128]{3,2,1,0:T(8,128)}), f32[16,4,8,128]{3,2,1,0:T(8,128)S(1)}, u32[]{:S(2)}, u32[]{:S(2)}) async-start(f32[16,4,8,128]{3,2,1,0:T(8,128)} %stack.54), calls=%async_computation.11 | async-start | bytes 524288 | tf_op jit(solution)/shard_map/all_to_all | solution.py:73
  595.7 114.0 %reduce-scatter.2.cloned.1.call-start = ((), (), s32[]{:S(2)}) async-start(), calls=%async_computation.14 | async-start | bytes 294912 | tf_op jit(solution)/shard_map/reduce_scatter | solution.py:131
  653.0 19.4 %collective-permute-start.26 = (f32[4,8,64]{2,1,0:T(8,128)S(1)}, f32[4,8,64]{2,1,0:T(8,128)S(1)}, u32[]{:S(2)}, u32[]{:S(2)}) collective-permute-start(f32[4,8,64]{2,1,0:T(8,128)S(1)} %bitcast.175), channel_id=1, source_target_pairs={{0,120},{8,0},{16,8},{24,16},{32,24},{40,32},{48,40},{56,48},{64,5... | collective-permute-start | bytes 24584 | tf_op jit(solution)/shard_map/ppermute | solution.py:34
  653.1 17.5 %collective-permute-start.27 = (f32[4,8,64]{2,1,0:T(8,128)S(1)}, f32[4,8,64]{2,1,0:T(8,128)S(1)}, u32[]{:S(2)}, u32[]{:S(2)}) collective-permute-start(f32[4,8,64]{2,1,0:T(8,128)S(1)} %bitcast.177), channel_id=1, source_target_pairs={{0,8},{8,16},{16,24},{24,32},{32,40},{40,48},{48,56},{56,64},{64,7... | collective-permute-start | bytes 24584 | tf_op jit(solution)/shard_map/ppermute | solution.py:34
  661.4 40.2 %all-to-all-start.12 = ((f32[16,4,8,128]{3,2,1,0:T(8,128)}), f32[16,4,8,128]{3,2,1,0:T(8,128)S(1)}, u32[]{:S(2)}, u32[]{:S(2)}) async-start(f32[16,4,8,128]{3,2,1,0:T(8,128)} %stack.56), calls=%async_computation.12 | async-start | bytes 524288 | tf_op jit(solution)/shard_map/all_to_all | solution.py:73
  (45 other events, 247.5 us)
Sparse Core Ops, SparseCore 0:
  660.8 37.7 reduce-scatter.1
